TPU v7x, 256 devices: a whole 4x4x8 slice. The times are simulated.
256 devices in a mesh: tm: 16 (over x, y), line: 16 (over z, core).
Axes of the slice: x: 4, y: 4, z: 8, core: 2. Of those that a mesh axis runs over, the one named last changes fastest.
Arguments:
- station_traces: bfloat16 [512, 65536], P('line', 'tm'), may hold values from -6 to 6
- shot_onset_ticks: int32 [256], P('line'), may hold values from 0 to 65535, as said below
- span_place_index: int32 [256], P('line'), may hold values from 0 to 31, as said below
- spectral_keep_flags: int32 [256, 512], replicated, may hold values 0 or 1
Outputs:
- deblended: bfloat16 [512, 512, 1024], P('tm', 'line')
Inputs may be any that keep to these rules, and one draw needn't show every extreme that they name: The block of 4096 samples holding shot_onset_ticks[s] owns shot s; each block owns at most 32 shots and one owns exactly 32. `span_place_index`: shots owned by the same block have distinct slots.
All inputs are finite; a program needn't handle non-finite values.
Results may differ from a plain program's by a relative error of at most 0.0078.
Values may be sent and summed in bfloat16 or wider, within the bound.
A program may use at most 64 MiB of HBM per device.

v0:
```python
import functools

import jax
import jax.numpy as jnp
import ml_dtypes
import numpy as np
from jax import lax
from jax.experimental import pallas as pl
from jax.experimental.pallas import tpu as pltpu
from jax.sharding import PartitionSpec as P

MESH = pl.DeviceIdType.MESH
LANES = 128
VMEM_LIMIT = 56 << 20
NT = (((1,), (1,)), ((), ()))


def make_tables(window, shots):
    freqs = window // 2
    phase = (np.outer(np.arange(window), np.arange(freqs)) % window) * (2.0 * np.pi / window)
    forward = np.concatenate([np.cos(phase), -np.sin(phase)], axis=1)
    angle = (np.outer(np.arange(shots), np.arange(shots)) % shots) * (2.0 * np.pi / shots)
    turn = np.concatenate([np.cos(angle), np.sin(angle)], axis=1)
    return (
        forward.astype(np.float32).astype(ml_dtypes.bfloat16),
        turn.astype(np.float32).astype(ml_dtypes.bfloat16),
    )


def torus_offsets(side):
    def hops(offset):
        return sum(min(step, side - step) for step in offset)

    every = [(dx, dy) for dx in range(side) for dy in range(side)]
    return sorted(every, key=hops)[1:]


def tm_peer(me, side, offset, sign=1):
    dx, dy = offset
    row = lax.rem(me // side + sign * dx + side, side)
    column = lax.rem(me % side + sign * dy + side, side)
    return row * side + column


def exchange_kernel(
    tm_count, line_count, side,
    blocks_ref, onset_ref, place_ref,
    records_ref, meta_ref,
    mine_ref, heard_ref, own_sem, tm_send, tm_recv, line_send, line_recv,
):
    me, line = lax.axis_index("tm"), lax.axis_index("line")
    offsets = torus_offsets(side)
    rows = blocks_ref.shape[1]
    local_shots = onset_ref.shape[0]
    barrier = pltpu.get_barrier_semaphore()
    for offset in offsets:
        pl.semaphore_signal(
            barrier, inc=1, device_id={"tm": tm_peer(me, side, offset, -1)}, device_id_type=MESH
        )
    for step in range(1, line_count):
        pl.semaphore_signal(
            barrier, inc=1, device_id={"line": lax.rem(line + step, line_count)}, device_id_type=MESH
        )
    shape = mine_ref.shape
    lane = lax.broadcasted_iota(jnp.int32, shape, 1) - line * local_shots
    first_row = lax.broadcasted_iota(jnp.int32, shape, 0) == 0
    mine = jnp.zeros(shape, jnp.int32)
    for i in range(local_shots):
        mine = jnp.where(lane == i, jnp.where(first_row, onset_ref[i], place_ref[i]), mine)
    mine_ref[...] = mine
    heard_ref[0] = mine
    own = pltpu.make_async_copy(
        blocks_ref.at[me], records_ref.at[pl.ds(pl.multiple_of(me * rows, rows), rows)], own_sem
    )
    own.start()
    pl.semaphore_wait(barrier, len(offsets) + line_count - 1)
    copies = []
    for step in range(1, line_count):
        copies.append(
            pltpu.make_async_remote_copy(
                mine_ref, heard_ref.at[step], line_send.at[step], line_recv.at[step],
                device_id={"line": lax.rem(line + step, line_count)}, device_id_type=MESH,
            )
        )
        copies[-1].start()
    for i, offset in enumerate(offsets):
        peer = tm_peer(me, side, offset)
        copies.append(
            pltpu.make_async_remote_copy(
                blocks_ref.at[peer],
                records_ref.at[pl.ds(pl.multiple_of(me * rows, rows), rows)],
                tm_send.at[i], tm_recv.at[i],
                device_id={"tm": peer}, device_id_type=MESH,
            )
        )
        copies[-1].start()
    own.wait()
    for copy in copies[: line_count - 1]:
        copy.wait()
    total = heard_ref[0]
    for step in range(1, line_count):
        total = total + heard_ref[step]
    meta_ref[...] = total
    for copy in copies[line_count - 1 :]:
        copy.wait()


def exchange(blocks, onsets, places, tm_count, line_count):
    side = int(round(tm_count**0.5))
    shots = onsets.shape[0] * line_count
    dma = pltpu.SemaphoreType.DMA
    return pl.pallas_call(
        functools.partial(exchange_kernel, tm_count, line_count, side),
        out_shape=(
            jax.ShapeDtypeStruct((tm_count * blocks.shape[1], LANES), jnp.bfloat16),
            jax.ShapeDtypeStruct((8, shots), jnp.int32),
        ),
        in_specs=[
            pl.BlockSpec(memory_space=pltpu.VMEM),
            pl.BlockSpec(memory_space=pltpu.SMEM),
            pl.BlockSpec(memory_space=pltpu.SMEM),
        ],
        out_specs=(
            pl.BlockSpec(memory_space=pltpu.VMEM),
            pl.BlockSpec(memory_space=pltpu.VMEM),
        ),
        scratch_shapes=[
            pltpu.VMEM((8, shots), jnp.int32),
            pltpu.VMEM((line_count, 8, shots), jnp.int32),
            dma, dma((tm_count,)), dma((tm_count,)), dma((line_count,)), dma((line_count,)),
        ],
        compiler_params=pltpu.CompilerParams(
            collective_id=0, has_side_effects=True, vmem_limit_bytes=8 << 20
        ),
        name="exchange_records",
    )(blocks, onsets, places)


def filter_kernel(
    block_len, capacity,
    onset_ref, meta_ref, records_ref, keep_ref, forward_hbm, turn_ref,
    mixed_ref,
    wide_ref, cut_ref, panels_ref, spectrum_ref, chosen_ref, forward_ref, sem,
):
    shots, freqs = keep_ref.shape
    window = 2 * freqs
    chunks = window // LANES
    pair = 2
    per_shot = pair * chunks
    record_rows = records_ref.shape[0]
    load = pltpu.make_async_copy(forward_hbm, forward_ref, sem)
    load.start()
    wide_ref[:record_rows] = records_ref[...].astype(jnp.float32)
    wide_ref[record_rows:] = jnp.zeros(
        (wide_ref.shape[0] - record_rows, LANES), jnp.float32
    )
    lane = lax.broadcasted_iota(jnp.int32, (per_shot, LANES), 1)

    def cut(shot):
        start = onset_ref[0, shot]
        base = (start // LANES) * pair
        within = lax.rem(start, LANES)
        here = wide_ref[pl.ds(base, per_shot), :]
        following = wide_ref[pl.ds(base + pair, per_shot), :]
        both = jnp.where(lane >= within, here, following)
        turned = pltpu.roll(both, lax.rem(LANES - within, LANES), 1)
        cut_ref[pl.ds(pl.multiple_of(shot * per_shot, per_shot), per_shot), :] = turned

    group = 8

    @pl.loop(0, shots // group)
    def _(step):
        for i in range(group):
            cut(step * group + i)

    for rec in range(pair):
        for chunk in range(chunks):
            panels_ref[rec * shots : (rec + 1) * shots, chunk * LANES : (chunk + 1) * LANES] = (
                cut_ref[pl.ds(pair * chunk + rec, shots, stride=per_shot), :].astype(jnp.bfloat16)
            )
    load.wait()
    width = 256

    @pl.loop(0, window // width)
    def _(step):
        columns = pl.ds(pl.multiple_of(step * width, width), width)
        spectrum_ref[:, columns] = jnp.dot(
            panels_ref[...], forward_ref[:, columns], preferred_element_type=jnp.float32
        ).astype(jnp.bfloat16)

    code = (meta_ref[0:1, :] // block_len) * capacity + meta_ref[1:2, :]
    slots = chosen_ref.shape[0]
    picked = (lax.broadcasted_iota(jnp.int32, (slots, shots), 0) == code).astype(jnp.float32)
    chosen_ref[...] = jnp.dot(
        picked.astype(jnp.bfloat16), turn_ref[...], preferred_element_type=jnp.float32
    ).astype(jnp.bfloat16)
    owners = slots // capacity
    half = jnp.float32(0.5)

    @pl.loop(0, pair * (freqs // width))
    def _(step):
        rec = step // (freqs // width)
        part = lax.rem(step, freqs // width)
        low = pl.ds(pl.multiple_of(part * width, width), width)
        high = pl.ds(pl.multiple_of(freqs + part * width, width), width)
        rows = pl.ds(pl.multiple_of(rec * shots, shots), shots)
        a, b = spectrum_ref[rows, low], spectrum_ref[rows, high]
        keep = keep_ref[:, low].astype(jnp.float32)
        turn = turn_ref[...]
        p = jnp.dot(turn, jnp.concatenate([a, b], axis=0), preferred_element_type=jnp.float32)
        q = jnp.dot(turn, jnp.concatenate([b, -a], axis=0), preferred_element_type=jnp.float32)
        p, q = (p * keep).astype(jnp.bfloat16), (q * keep).astype(jnp.bfloat16)
        chosen = chosen_ref[...]
        ma = jnp.dot(chosen, jnp.concatenate([p, -q], axis=0), preferred_element_type=jnp.float32)
        mb = jnp.dot(chosen, jnp.concatenate([q, p], axis=0), preferred_element_type=jnp.float32)
        first = lax.broadcasted_iota(jnp.int32, (slots, width), 1) + part * width == 0
        ma = jnp.where(first, ma * half, ma).astype(jnp.bfloat16)
        mb = jnp.where(first, mb * half, mb).astype(jnp.bfloat16)
        for owner in range(owners):
            mine = slice(owner * capacity, (owner + 1) * capacity)
            there = pl.ds(pl.multiple_of(rec * capacity, capacity), capacity)
            mixed_ref[owner, there, low] = ma[mine]
            mixed_ref[owner, there, high] = mb[mine]


def filter_records(meta, records, keep_flags, forward, turn, tm_count, block_len):
    shots, freqs = keep_flags.shape
    window = 2 * freqs
    capacity = 2 * shots // tm_count
    vmem = pl.BlockSpec(memory_space=pltpu.VMEM)
    return pl.pallas_call(
        functools.partial(filter_kernel, block_len, capacity),
        out_shape=jax.ShapeDtypeStruct((tm_count, 2 * capacity, window), jnp.bfloat16),
        in_specs=[
            pl.BlockSpec(memory_space=pltpu.SMEM), vmem, vmem, vmem,
            pl.BlockSpec(memory_space=pl.ANY), vmem,
        ],
        out_specs=vmem,
        scratch_shapes=[
            pltpu.VMEM((records.shape[0] + 4 * window // LANES, LANES), jnp.float32),
            pltpu.VMEM((2 * shots * window // LANES, LANES), jnp.float32),
            pltpu.VMEM((2 * shots, window), jnp.bfloat16),
            pltpu.VMEM((2 * shots, window), jnp.bfloat16),
            pltpu.VMEM((tm_count * capacity, 2 * shots), jnp.bfloat16),
            pltpu.VMEM((window, window), jnp.bfloat16),
            pltpu.SemaphoreType.DMA,
        ],
        compiler_params=pltpu.CompilerParams(vmem_limit_bytes=VMEM_LIMIT),
        name="filter_records",
    )(meta, meta, records, keep_flags, forward, turn)


def deliver_kernel(
    tm_count, side, batch,
    mixed_ref, forward_hbm,
    traces_ref,
    arrived_ref, forward_ref, load_sem, own_sem, send_sem, recv_sem,
):
    me = lax.axis_index("tm")
    offsets = [(0, 0)] + torus_offsets(side)
    rows = mixed_ref.shape[1]
    capacity = rows // 2
    window = mixed_ref.shape[2]
    load = pltpu.make_async_copy(forward_hbm, forward_ref, load_sem)
    load.start()
    barrier = pltpu.get_barrier_semaphore()
    for offset in offsets[1:]:
        pl.semaphore_signal(
            barrier, inc=1, device_id={"tm": tm_peer(me, side, offset, -1)}, device_id_type=MESH
        )
    own = pltpu.make_async_copy(mixed_ref.at[me], arrived_ref.at[0], own_sem)
    own.start()
    pl.semaphore_wait(barrier, tm_count - 1)
    copies = [own]
    for i, offset in enumerate(offsets):
        if i == 0:
            continue
        peer = tm_peer(me, side, offset)
        copies.append(
            pltpu.make_async_remote_copy(
                mixed_ref.at[peer], arrived_ref.at[i], send_sem.at[i], recv_sem.at[i],
                device_id={"tm": peer}, device_id_type=MESH,
            )
        )
        copies[-1].start()
    load.wait()
    width = 256
    scale = jnp.float32(4.0 / (window * tm_count * capacity))
    for first in range(0, tm_count, batch):
        for i in range(first, first + batch):
            if i == 0:
                own.wait()
            else:
                copies[i].wait_recv()
        sources = [tm_peer(me, side, offsets[i], -1) for i in range(first, first + batch)]

        @pl.loop(0, window // width)
        def _(step):
            columns = pl.ds(pl.multiple_of(step * width, width), width)
            block = arrived_ref[first : first + batch].reshape(batch * rows, window)
            out = lax.dot_general(
                block, forward_ref[columns, :], NT, preferred_element_type=jnp.float32
            ) * scale
            for i in range(batch):
                for rec in range(2):
                    at = i * rows + rec * capacity
                    for tile in range(width // LANES):
                        traces_ref[
                            step * (width // LANES) + tile,
                            pl.ds(sources[i] * 2 + rec, capacity, stride=2 * tm_count),
                            :,
                        ] = out[at : at + capacity, tile * LANES : (tile + 1) * LANES]

    for copy in copies[1:]:
        copy.wait_send()


def deliver(mixed, forward, batch=4):
    tm_count, rows, window = mixed.shape
    side = int(round(tm_count**0.5))
    dma = pltpu.SemaphoreType.DMA
    return pl.pallas_call(
        functools.partial(deliver_kernel, tm_count, side, batch),
        out_shape=jax.ShapeDtypeStruct((window // LANES, tm_count * rows, LANES), jnp.float32),
        in_specs=[
            pl.BlockSpec(memory_space=pltpu.VMEM),
            pl.BlockSpec(memory_space=pl.ANY),
        ],
        out_specs=pl.BlockSpec(memory_space=pltpu.VMEM),
        scratch_shapes=[
            pltpu.VMEM(mixed.shape, jnp.bfloat16),
            pltpu.VMEM(forward.shape, jnp.bfloat16),
            dma, dma, dma((tm_count,)), dma((tm_count,)),
        ],
        compiler_params=pltpu.CompilerParams(
            collective_id=1, has_side_effects=True, vmem_limit_bytes=VMEM_LIMIT
        ),
        name="deliver_windows",
    )(mixed, forward)


def on_device(station_traces, shot_onset_ticks, span_place_index, spectral_keep_flags):
    tm_count, line_count = lax.axis_size("tm"), lax.axis_size("line")
    rec_rows, block_len = station_traces.shape
    shots, freqs = spectral_keep_flags.shape
    window = 2 * freqs
    forward, turn = make_tables(window, shots)
    forward, turn = jnp.asarray(forward), jnp.asarray(turn)
    blocks = station_traces.reshape(tm_count, rec_rows // tm_count, block_len // LANES, LANES)
    blocks = jnp.swapaxes(blocks, 1, 2).reshape(tm_count, -1, LANES)
    records, meta = exchange(blocks, shot_onset_ticks, span_place_index, tm_count, line_count)
    mixed = filter_records(
        meta, records, spectral_keep_flags, forward, turn, tm_count, block_len
    )
    traces = deliver(mixed, forward)
    traces = jnp.swapaxes(traces.astype(jnp.bfloat16), 0, 1)
    return traces.reshape(2 * shots // tm_count, rec_rows, window)


def solution(mesh):
    in_specs = (P("line", "tm"), P("line"), P("line"), P())
    out_specs = P("tm", "line", None)
    return jax.shard_map(
        on_device, mesh=mesh, in_specs=in_specs, out_specs=out_specs, check_vma=False
    )
```

profile of v0, /device:TPU:8, one launch (start us, length us, event | category | flops | bytes accessed | tf_op | source)
XLA Modules:
  0.0 74.2 jit_solution(6729230856622115629)
XLA Ops:
  0.0 1.0 %copy.10 = bf16[4,8,32,128]{3,2,1,0:T(8,128)(2,1)S(1)} copy(bf16[4,8,32,128]{3,1,2,0:T(8,128)(2,1)} %bitcast.10) | data formatting | bytes 524288
  1.0 0.2 copy.8
  1.2 0.0 copy-start.2
  1.3 0.6 copy-done.2
  1.9 0.0 copy-start.3
  1.9 0.7 copy-done.3
  2.6 17.1 %exchange_records.1 = (bf16[1024,128]{1,0:T(8,128)(2,1)S(1)}, s32[8,256]{1,0:T(8,128)S(1)}) custom-call(bf16[16,64,128]{2,1,0:T(8,128)(2,1)S(1)} %bitcast.8, s32[16]{0:T(128)S(1)} %copy-done.2, s32[16]{0:T(128)S(1)} %copy-done.3), custom_call_target="tpu_custom_call" | custom-call | tf_op jit(solution)/shard_map/exchange_records/pallas_call | solution.py:112
  19.7 0.0 copy-start
  19.7 0.7 copy-done
  20.4 0.0 copy-start.1
  20.4 0.6 copy-done.1
  20.9 12.0 %filter_records.1.mixed_ref = bf16[16,64,1024]{2,1,0:T(8,128)(2,1)} custom-call(s32[8,256]{1,0:T(8,128)} %copy-done.1, s32[8,256]{1,0:T(8,128)} %copy-done.1, bf16[1024,128]{1,0:T(8,128)(2,1)} %copy-done, s32[256,512]{1,0:T(8,128)} %keep_ref.1, bf16[1024,1024]{1,0:T(8,128)(2,1)} %constant.4.clone.forward_hbm, bf16[256,512]{1,0:T(8,128)(2,1)} %constant.5.clone.turn_ref), custom_call_target="tpu_custom_call" | custom-call | tf_op jit(solution)/shard_map/filter_records/pallas_call | solution.py:231
  32.9 35.1 %deliver_windows.1 = f32[8,1024,128]{2,1,0:T(8,128)} custom-call(bf16[16,64,1024]{2,1,0:T(8,128)(2,1)} %filter_records.1.mixed_ref, bf16[1024,1024]{1,0:T(8,128)(2,1)} %constant.4.clone.forward_hbm), custom_call_target="tpu_custom_call" | custom-call | tf_op jit(solution)/shard_map/deliver_windows/pallas_call | solution.py:322
  68.0 2.5 %convert_bitcast_fusion = bf16[1024,8,128]{2,0,1:T(8,128)(2,1)S(1)} fusion(f32[8,1024,128]{2,1,0:T(8,128)} %deliver_windows.1), kind=kLoop, calls=%fused_computation | loop fusion | flops 1048576 | bytes 6291456 | tf_op jit(solution)/shard_map/transpose | solution.py:356
  70.6 1.4 %copy.9 = bf16[1024,8,128]{2,1,0:T(8,128)(2,1)S(1)} copy(bf16[1024,8,128]{2,0,1:T(8,128)(2,1)S(1)} %convert_bitcast_fusion) | data formatting | bytes 4194304 | tf_op jit(solution)/shard_map/transpose | solution.py:356
  71.9 2.3 %reshape.11 = bf16[32,32,1024]{2,1,0:T(8,128)(2,1)} reshape(bf16[1024,8,128]{2,1,0:T(8,128)(2,1)S(1)} %copy.9) | data formatting | bytes 4194304 | tf_op jit(solution)/shard_map/reshape | solution.py:357
Async XLA Ops:
  1.2 0.7 copy-start.2
  1.9 0.7 copy-start.3
  19.7 0.7 copy-start
  20.4 0.6 copy-start.1
where the time goes:
time: 74.4 us; the launch traced here: 74.2 us
  Pallas kernels  64.2 us (86%)
  local copies, waits for them, and re-layouts  7.46 us (10%)
  other arithmetic  2.52 us (3%)
    pallas_call x1, Pallas kernels, deliver(): pl.pallas_call(functools.partial(deliver_kernel, tm_count, side, batch),...  35.1 us
    pallas_call x1, Pallas kernels, exchange(): pl.pallas_call(functools.partial(exchange_kernel, tm_count, line_count, s...  17.1 us
    pallas_call x1, Pallas kernels, filter_records(): pl.pallas_call(functools.partial(filter_kernel, block_len, capacity), out...  12 us
    unnamed x9, local copies, waits for them, and re-layouts  3.57 us
    transpose x1, other arithmetic, on_device(): traces = jnp.swapaxes(traces.astype(jnp.bfloat16), 0, 1)  2.52 us
    reshape x1, local copies, waits for them, and re-layouts, on_device(): return traces.reshape(2 * shots // tm_count, rec_rows, window)  2.29 us

commit v1 on v0

--- a/solution.py
+++ b/solution.py
@@ -11,7 +11,6 @@
 
 MESH = pl.DeviceIdType.MESH
 LANES = 128
-VMEM_LIMIT = 56 << 20
 NT = (((1,), (1,)), ((), ()))
 
 
@@ -245,7 +244,7 @@
             pltpu.VMEM((window, window), jnp.bfloat16),
             pltpu.SemaphoreType.DMA,
         ],
-        compiler_params=pltpu.CompilerParams(vmem_limit_bytes=VMEM_LIMIT),
+        compiler_params=pltpu.CompilerParams(vmem_limit_bytes=24 << 20),
         name="filter_records",
     )(meta, meta, records, keep_flags, forward, turn)
 
@@ -333,10 +332,44 @@
             dma, dma, dma((tm_count,)), dma((tm_count,)),
         ],
         compiler_params=pltpu.CompilerParams(
-            collective_id=1, has_side_effects=True, vmem_limit_bytes=VMEM_LIMIT
+            collective_id=1, has_side_effects=True, vmem_limit_bytes=24 << 20
         ),
         name="deliver_windows",
     )(mixed, forward)
+
+
+def place_kernel(traces_ref, placed_ref, staged_ref, sem):
+    slots, receivers, _ = staged_ref.shape
+
+    def out_copy(slot):
+        return pltpu.make_async_copy(staged_ref.at[slot], placed_ref.at[slot], sem.at[slot])
+
+    @pl.loop(0, slots)
+    def _(slot):
+        for tile in range(traces_ref.shape[0]):
+            rows = traces_ref[tile, pl.ds(pl.multiple_of(slot * receivers, receivers), receivers), :]
+            staged_ref[slot, :, tile * LANES : (tile + 1) * LANES] = rows.astype(jnp.bfloat16)
+        out_copy(slot).start()
+
+    @pl.loop(0, slots)
+    def _(slot):
+        out_copy(slot).wait()
+
+
+def place(traces, slots, receivers):
+    window = traces.shape[0] * LANES
+    return pl.pallas_call(
+        place_kernel,
+        out_shape=jax.ShapeDtypeStruct((slots, receivers, window), jnp.bfloat16),
+        in_specs=[pl.BlockSpec(memory_space=pltpu.VMEM)],
+        out_specs=pl.BlockSpec(memory_space=pl.ANY),
+        scratch_shapes=[
+            pltpu.VMEM((slots, receivers, window), jnp.bfloat16),
+            pltpu.SemaphoreType.DMA((slots,)),
+        ],
+        compiler_params=pltpu.CompilerParams(vmem_limit_bytes=12 << 20),
+        name="place_windows",
+    )(traces)
 
 
 def on_device(station_traces, shot_onset_ticks, span_place_index, spectral_keep_flags):
@@ -353,8 +386,7 @@
         meta, records, spectral_keep_flags, forward, turn, tm_count, block_len
     )
     traces = deliver(mixed, forward)
-    traces = jnp.swapaxes(traces.astype(jnp.bfloat16), 0, 1)
-    return traces.reshape(2 * shots // tm_count, rec_rows, window)
+    return place(traces, 2 * shots // tm_count, rec_rows)
 
 
 def solution(mesh):

time: 74.4 us -> 67.2 us (0.903)
  Pallas kernels: 64.2 us -> 60.7 us
  other arithmetic: 2.52 us -> 0 us
  local copies, waits for them, and re-layouts: 7.46 us -> 6.11 us
    pallas_call x1, Pallas kernels: 35.1 us -> 31.8 us  [deliver(): pl.pallas_call(functools.partial(deliver_kernel, tm_count, side, batch),...]
    transpose x1 -> x0, other arithmetic: 2.52 us -> none  [on_device(): traces = jnp.swapaxes(traces.astype(jnp.bfloat16), 0, 1)]
    unnamed x9 -> x13, local copies, waits for them, and re-layouts: 3.57 us -> 5.88 us
    reshape x1 -> x0, local copies, waits for them, and re-layouts: 2.29 us -> none  [on_device(): return traces.reshape(2 * shots // tm_count, rec_rows, window)]
    pallas_call x1, Pallas kernels: 12 us -> 10.2 us  [filter_records(): pl.pallas_call(functools.partial(filter_kernel, block_len, capacity), out...]
    pallas_call x0 -> x1, Pallas kernels: none -> 1.58 us  [place(): pl.pallas_call(place_kernel, out_shape=jax.ShapeDtypeStruct((slots, recei...]
    transpose x1 -> x0, local copies, waits for them, and re-layouts: 1.35 us -> none  [on_device(): traces = jnp.swapaxes(traces.astype(jnp.bfloat16), 0, 1)]
where the time goes in v1:
time: 67.2 us; the launch traced here: 66.9 us
  Pallas kernels  60.7 us (90%)
  local copies, waits for them, and re-layouts  6.11 us (9%)
    pallas_call x1, Pallas kernels, deliver(): pl.pallas_call(functools.partial(deliver_kernel, tm_count, side, batch),...  31.8 us
    pallas_call x1, Pallas kernels, exchange(): pl.pallas_call(functools.partial(exchange_kernel, tm_count, line_count, s...  17.1 us
    pallas_call x1, Pallas kernels, filter_records(): pl.pallas_call(functools.partial(filter_kernel, block_len, capacity), out...  10.2 us
    unnamed x13, local copies, waits for them, and re-layouts  5.88 us
    pallas_call x1, Pallas kernels, place(): pl.pallas_call(place_kernel, out_shape=jax.ShapeDtypeStruct((slots, recei...  1.58 us

profile of v1, /device:TPU:8, one launch (start us, length us, event | category | flops | bytes accessed | tf_op | source)
XLA Modules:
  0.0 66.9 jit_solution(3542960873636880517)
XLA Ops:
  0.0 1.0 %copy.8 = bf16[4,8,32,128]{3,2,1,0:T(8,128)(2,1)S(1)} copy(bf16[4,8,32,128]{3,1,2,0:T(8,128)(2,1)} %bitcast.8) | data formatting | bytes 524288
  1.0 0.2 copy.7
  1.2 0.0 copy-start.4
  1.3 0.6 copy-done.4
  1.9 0.0 copy-start.5
  1.9 0.7 copy-done.5
  2.6 17.1 %exchange_records.1 = (bf16[1024,128]{1,0:T(8,128)(2,1)S(1)}, s32[8,256]{1,0:T(8,128)S(1)}) custom-call(bf16[16,64,128]{2,1,0:T(8,128)(2,1)S(1)} %bitcast.6, s32[16]{0:T(128)S(1)} %copy-done.4, s32[16]{0:T(128)S(1)} %copy-done.5), custom_call_target="tpu_custom_call" | custom-call | tf_op jit(solution)/shard_map/exchange_records/pallas_call | solution.py:111
  19.7 0.0 copy-start
  19.7 1.6 %copy-done = bf16[1024,1024]{1,0:T(8,128)(2,1)S(1)} copy-done((bf16[1024,1024]{1,0:T(8,128)(2,1)S(1)}, bf16[1024,1024]{1,0:T(8,128)(2,1)}, u32[]{:S(2)}) %copy-start) | copy-done | bytes 2097176
  21.3 0.0 copy-start.2
  21.3 1.0 %copy-done.2 = s32[256,512]{1,0:T(8,128)S(1)} copy-done((s32[256,512]{1,0:T(8,128)S(1)}, s32[256,512]{1,0:T(8,128)}, u32[]{:S(2)}) %copy-start.2) | copy-done | bytes 524312
  22.3 0.0 copy-start.3
  22.3 0.9 %copy-done.3 = bf16[256,512]{1,0:T(8,128)(2,1)S(1)} copy-done((bf16[256,512]{1,0:T(8,128)(2,1)S(1)}, bf16[256,512]{1,0:T(8,128)(2,1)}, u32[]{:S(2)}) %copy-start.3) | copy-done | bytes 262168
  23.2 0.0 copy-start.1
  23.2 10.2 %filter_records.1.mixed_ref = bf16[16,64,1024]{2,1,0:T(8,128)(2,1)S(1)} custom-call(s32[8,256]{1,0:T(8,128)S(1)} %get-tuple-element.7.onset_ref.meta_ref, s32[8,256]{1,0:T(8,128)S(1)} %get-tuple-element.7.onset_ref.meta_ref, bf16[1024,128]{1,0:T(8,128)(2,1)S(1)} %get-tuple-element.8.records_ref, s32[256,512]{1,0:T(8,128)S(1)} %copy-done.2, ...), custom_call_target="tpu_custom_call" | custom-call | tf_op jit(solution)/shard_map/filter_records/pallas_call | solution.py:230
  33.5 0.0 copy-done.1
  33.5 31.8 %deliver_windows.1.traces_ref = f32[8,1024,128]{2,1,0:T(8,128)S(1)} custom-call(bf16[16,64,1024]{2,1,0:T(8,128)(2,1)S(1)} %filter_records.1.mixed_ref, bf16[1024,1024]{1,0:T(8,128)(2,1)S(1)} %copy-done.1), custom_call_target="tpu_custom_call" | custom-call | tf_op jit(solution)/shard_map/deliver_windows/pallas_call | solution.py:321
  65.4 1.6 %place_windows.1 = bf16[32,32,1024]{2,1,0:T(8,128)(2,1)} custom-call(f32[8,1024,128]{2,1,0:T(8,128)S(1)} %deliver_windows.1.traces_ref), custom_call_target="tpu_custom_call" | custom-call | tf_op jit(solution)/shard_map/place_windows/pallas_call | solution.py:361
Async XLA Ops:
  1.2 0.7 copy-start.4
  1.9 0.7 copy-start.5
  19.7 1.6 %copy-start = (bf16[1024,1024]{1,0:T(8,128)(2,1)S(1)}, bf16[1024,1024]{1,0:T(8,128)(2,1)}, u32[]{:S(2)}) copy-start(bf16[1024,1024]{1,0:T(8,128)(2,1)} %constant.4.clone.forward_hbm) | copy-start | bytes 6291460
  21.3 1.0 %copy-start.2 = (s32[256,512]{1,0:T(8,128)S(1)}, s32[256,512]{1,0:T(8,128)}, u32[]{:S(2)}) copy-start(s32[256,512]{1,0:T(8,128)} %keep_ref.1) | copy-start | bytes 1572868
  22.3 0.9 %copy-start.3 = (bf16[256,512]{1,0:T(8,128)(2,1)S(1)}, bf16[256,512]{1,0:T(8,128)(2,1)}, u32[]{:S(2)}) copy-start(bf16[256,512]{1,0:T(8,128)(2,1)} %constant.5.clone.turn_ref) | copy-start | bytes 786436
  23.2 10.2 %copy-start.1 = (bf16[1024,1024]{1,0:T(8,128)(2,1)S(1)}, bf16[1024,1024]{1,0:T(8,128)(2,1)}, u32[]{:S(2)}) copy-start(bf16[1024,1024]{1,0:T(8,128)(2,1)} %constant.4.clone.forward_hbm) | copy-start | bytes 6291460

commit v2 on v1

--- a/solution.py
+++ b/solution.py
@@ -43,9 +43,9 @@
 
 def exchange_kernel(
     tm_count, line_count, side,
-    blocks_ref, onset_ref, place_ref,
-    records_ref, meta_ref,
-    mine_ref, heard_ref, own_sem, tm_send, tm_recv, line_send, line_recv,
+    blocks_ref, onset_ref, place_ref, forward_hbm, turn_hbm, keep_hbm,
+    records_ref, meta_ref, forward_ref, turn_ref, keep_ref,
+    mine_ref, heard_ref, own_sem, load_sem, tm_send, tm_recv, line_send, line_recv,
 ):
     me, line = lax.axis_index("tm"), lax.axis_index("line")
     offsets = torus_offsets(side)
@@ -60,6 +60,14 @@
         pl.semaphore_signal(
             barrier, inc=1, device_id={"line": lax.rem(line + step, line_count)}, device_id_type=MESH
         )
+    loads = [
+        pltpu.make_async_copy(there, here, load_sem.at[i])
+        for i, (there, here) in enumerate(
+            ((forward_hbm, forward_ref), (turn_hbm, turn_ref), (keep_hbm, keep_ref))
+        )
+    ]
+    for load in loads:
+        load.start()
     shape = mine_ref.shape
     lane = lax.broadcasted_iota(jnp.int32, shape, 1) - line * local_shots
     first_row = lax.broadcasted_iota(jnp.int32, shape, 0) == 0
@@ -102,9 +110,11 @@
     meta_ref[...] = total
     for copy in copies[line_count - 1 :]:
         copy.wait()
-
-
-def exchange(blocks, onsets, places, tm_count, line_count):
+    for load in loads:
+        load.wait()
+
+
+def exchange(blocks, onsets, places, tables, tm_count, line_count):
     side = int(round(tm_count**0.5))
     shots = onsets.shape[0] * line_count
     dma = pltpu.SemaphoreType.DMA
@@ -113,33 +123,32 @@
         out_shape=(
             jax.ShapeDtypeStruct((tm_count * blocks.shape[1], LANES), jnp.bfloat16),
             jax.ShapeDtypeStruct((8, shots), jnp.int32),
+            *(jax.ShapeDtypeStruct(table.shape, table.dtype) for table in tables),
         ),
         in_specs=[
             pl.BlockSpec(memory_space=pltpu.VMEM),
             pl.BlockSpec(memory_space=pltpu.SMEM),
             pl.BlockSpec(memory_space=pltpu.SMEM),
-        ],
-        out_specs=(
-            pl.BlockSpec(memory_space=pltpu.VMEM),
-            pl.BlockSpec(memory_space=pltpu.VMEM),
-        ),
+            *(pl.BlockSpec(memory_space=pl.ANY) for _ in tables),
+        ],
+        out_specs=tuple(pl.BlockSpec(memory_space=pltpu.VMEM) for _ in range(2 + len(tables))),
         scratch_shapes=[
             pltpu.VMEM((8, shots), jnp.int32),
             pltpu.VMEM((line_count, 8, shots), jnp.int32),
-            dma, dma((tm_count,)), dma((tm_count,)), dma((line_count,)), dma((line_count,)),
+            dma, dma((len(tables),)), dma((tm_count,)), dma((tm_count,)), dma((line_count,)), dma((line_count,)),
         ],
         compiler_params=pltpu.CompilerParams(
-            collective_id=0, has_side_effects=True, vmem_limit_bytes=8 << 20
+            collective_id=0, has_side_effects=True, vmem_limit_bytes=49 << 20
         ),
         name="exchange_records",
-    )(blocks, onsets, places)
+    )(blocks, onsets, places, *tables)
 
 
 def filter_kernel(
     block_len, capacity,
-    onset_ref, meta_ref, records_ref, keep_ref, forward_hbm, turn_ref,
+    onset_ref, meta_ref, records_ref, keep_ref, forward_ref, turn_ref,
     mixed_ref,
-    wide_ref, cut_ref, panels_ref, spectrum_ref, chosen_ref, forward_ref, sem,
+    wide_ref, cut_ref, panels_ref, spectrum_ref, chosen_ref,
 ):
     shots, freqs = keep_ref.shape
     window = 2 * freqs
@@ -147,8 +156,6 @@
     pair = 2
     per_shot = pair * chunks
     record_rows = records_ref.shape[0]
-    load = pltpu.make_async_copy(forward_hbm, forward_ref, sem)
-    load.start()
     wide_ref[:record_rows] = records_ref[...].astype(jnp.float32)
     wide_ref[record_rows:] = jnp.zeros(
         (wide_ref.shape[0] - record_rows, LANES), jnp.float32
@@ -177,7 +184,6 @@
             panels_ref[rec * shots : (rec + 1) * shots, chunk * LANES : (chunk + 1) * LANES] = (
                 cut_ref[pl.ds(pair * chunk + rec, shots, stride=per_shot), :].astype(jnp.bfloat16)
             )
-    load.wait()
     width = 256
 
     @pl.loop(0, window // width)
@@ -231,8 +237,7 @@
         functools.partial(filter_kernel, block_len, capacity),
         out_shape=jax.ShapeDtypeStruct((tm_count, 2 * capacity, window), jnp.bfloat16),
         in_specs=[
-            pl.BlockSpec(memory_space=pltpu.SMEM), vmem, vmem, vmem,
-            pl.BlockSpec(memory_space=pl.ANY), vmem,
+            pl.BlockSpec(memory_space=pltpu.SMEM), vmem, vmem, vmem, vmem, vmem,
         ],
         out_specs=vmem,
         scratch_shapes=[
@@ -241,8 +246,6 @@
             pltpu.VMEM((2 * shots, window), jnp.bfloat16),
             pltpu.VMEM((2 * shots, window), jnp.bfloat16),
             pltpu.VMEM((tm_count * capacity, 2 * shots), jnp.bfloat16),
-            pltpu.VMEM((window, window), jnp.bfloat16),
-            pltpu.SemaphoreType.DMA,
         ],
         compiler_params=pltpu.CompilerParams(vmem_limit_bytes=24 << 20),
         name="filter_records",
@@ -251,17 +254,15 @@
 
 def deliver_kernel(
     tm_count, side, batch,
-    mixed_ref, forward_hbm,
+    mixed_ref, forward_ref,
     traces_ref,
-    arrived_ref, forward_ref, load_sem, own_sem, send_sem, recv_sem,
+    arrived_ref, own_sem, send_sem, recv_sem,
 ):
     me = lax.axis_index("tm")
     offsets = [(0, 0)] + torus_offsets(side)
     rows = mixed_ref.shape[1]
     capacity = rows // 2
     window = mixed_ref.shape[2]
-    load = pltpu.make_async_copy(forward_hbm, forward_ref, load_sem)
-    load.start()
     barrier = pltpu.get_barrier_semaphore()
     for offset in offsets[1:]:
         pl.semaphore_signal(
@@ -282,7 +283,6 @@
             )
         )
         copies[-1].start()
-    load.wait()
     width = 256
     scale = jnp.float32(4.0 / (window * tm_count * capacity))
     for first in range(0, tm_count, batch):
@@ -323,13 +323,12 @@
         out_shape=jax.ShapeDtypeStruct((window // LANES, tm_count * rows, LANES), jnp.float32),
         in_specs=[
             pl.BlockSpec(memory_space=pltpu.VMEM),
-            pl.BlockSpec(memory_space=pl.ANY),
+            pl.BlockSpec(memory_space=pltpu.VMEM),
         ],
         out_specs=pl.BlockSpec(memory_space=pltpu.VMEM),
         scratch_shapes=[
             pltpu.VMEM(mixed.shape, jnp.bfloat16),
-            pltpu.VMEM(forward.shape, jnp.bfloat16),
-            dma, dma, dma((tm_count,)), dma((tm_count,)),
+            dma, dma((tm_count,)), dma((tm_count,)),
         ],
         compiler_params=pltpu.CompilerParams(
             collective_id=1, has_side_effects=True, vmem_limit_bytes=24 << 20
@@ -381,9 +380,12 @@
     forward, turn = jnp.asarray(forward), jnp.asarray(turn)
     blocks = station_traces.reshape(tm_count, rec_rows // tm_count, block_len // LANES, LANES)
     blocks = jnp.swapaxes(blocks, 1, 2).reshape(tm_count, -1, LANES)
-    records, meta = exchange(blocks, shot_onset_ticks, span_place_index, tm_count, line_count)
+    tables = (forward, turn, spectral_keep_flags)
+    records, meta, forward, turn, keep = exchange(
+        blocks, shot_onset_ticks, span_place_index, tables, tm_count, line_count
+    )
     mixed = filter_records(
-        meta, records, spectral_keep_flags, forward, turn, tm_count, block_len
+        meta, records, keep, forward, turn, tm_count, block_len
     )
     traces = deliver(mixed, forward)
     return place(traces, 2 * shots // tm_count, rec_rows)

time: 67.2 us -> 65.3 us (0.972)
  local copies, waits for them, and re-layouts: 6.11 us -> 4.52 us
    unnamed x13 -> x9, local copies, waits for them, and re-layouts: 5.88 us -> 4.29 us
where the time goes in v2:
time: 65.3 us; the launch traced here: 65.1 us
  Pallas kernels  60.5 us (93%)
  local copies, waits for them, and re-layouts  4.52 us (7%)
    pallas_call x1, Pallas kernels, deliver(): pl.pallas_call(functools.partial(deliver_kernel, tm_count, side, batch),...  31.7 us
    pallas_call x1, Pallas kernels, exchange(): pl.pallas_call(functools.partial(exchange_kernel, tm_count, line_count, s...  17.1 us
    pallas_call x1, Pallas kernels, filter_records(): pl.pallas_call(functools.partial(filter_kernel, block_len, capacity), out...  10.1 us
    unnamed x9, local copies, waits for them, and re-layouts  4.29 us
    pallas_call x1, Pallas kernels, place(): pl.pallas_call(place_kernel, out_shape=jax.ShapeDtypeStruct((slots, recei...  1.58 us

profile of v2, /device:TPU:8, one launch (start us, length us, event | category | flops | bytes accessed | tf_op | source)
XLA Modules:
  0.0 65.1 jit_solution(13845100060391436229)
XLA Ops:
  0.0 1.0 %copy.8 = bf16[4,8,32,128]{3,2,1,0:T(8,128)(2,1)S(1)} copy(bf16[4,8,32,128]{3,1,2,0:T(8,128)(2,1)} %bitcast.8) | data formatting | bytes 524288
  1.0 0.2 copy.7
  1.2 0.0 copy-start
  1.3 1.0 %copy-done = s32[256,512]{1,0:T(8,128)S(1)} copy-done((s32[256,512]{1,0:T(8,128)S(1)}, s32[256,512]{1,0:T(8,128)}, u32[]{:S(2)}) %copy-start) | copy-done | bytes 524312
  2.3 0.0 copy-start.1
  2.3 0.9 %copy-done.1 = bf16[256,512]{1,0:T(8,128)(2,1)S(1)} copy-done((bf16[256,512]{1,0:T(8,128)(2,1)S(1)}, bf16[256,512]{1,0:T(8,128)(2,1)}, u32[]{:S(2)}) %copy-start.1) | copy-done | bytes 262168
  3.2 0.0 copy-start.2
  3.2 0.7 %copy-done.2 = s32[16]{0:T(128)S(1)} copy-done((s32[16]{0:T(128)S(1)}, s32[16]{0:T(128)}, u32[]{:S(2)}) %copy-start.2) | copy-done | bytes 88
  3.9 0.0 copy-start.3
  3.9 0.7 %copy-done.3 = s32[16]{0:T(128)S(1)} copy-done((s32[16]{0:T(128)S(1)}, s32[16]{0:T(128)}, u32[]{:S(2)}) %copy-start.3) | copy-done | bytes 88
  4.6 17.1 %exchange_records.1 = (bf16[1024,128]{1,0:T(8,128)(2,1)S(1)}, s32[8,256]{1,0:T(8,128)S(1)}, bf16[1024,1024]{1,0:T(8,128)(2,1)S(1)}, bf16[256,512]{1,0:T(8,128)(2,1)S(1)}, s32[256,512]{1,0:T(8,128)S(1)}) custom-call(bf16[16,64,128]{2,1,0:T(8,128)(2,1)S(1)} %bitcast.6, s32[16]{0:T(128)S(1)} %copy-done.2, s32[16]{0:T(128)S(1)} %copy-done.3, ...), custom_call_target="tpu_custom_call" | custom-call | tf_op jit(solution)/shard_map/exchange_records/pallas_call | solution.py:121
  21.7 10.1 %filter_records.1.mixed_ref = bf16[16,64,1024]{2,1,0:T(8,128)(2,1)S(1)} custom-call(s32[8,256]{1,0:T(8,128)S(1)} %get-tuple-element.10.onset_ref.meta_ref, s32[8,256]{1,0:T(8,128)S(1)} %get-tuple-element.10.onset_ref.meta_ref, bf16[1024,128]{1,0:T(8,128)(2,1)S(1)} %get-tuple-element.11.records_ref, s32[256,512]{1,0:T(8,128)S(1)} %get-tuple-element.12.keep_ref, ...), custom_call_target="tpu_custom_call" | custom-call | tf_op jit(solution)/shard_map/filter_records/pallas_call | solution.py:236
  31.8 31.7 %deliver_windows.1.traces_ref = f32[8,1024,128]{2,1,0:T(8,128)S(1)} custom-call(bf16[16,64,1024]{2,1,0:T(8,128)(2,1)S(1)} %filter_records.1.mixed_ref, bf16[1024,1024]{1,0:T(8,128)(2,1)S(1)} %get-tuple-element.13.forward_ref), custom_call_target="tpu_custom_call" | custom-call | tf_op jit(solution)/shard_map/deliver_windows/pallas_call | solution.py:321
  63.5 1.6 %place_windows.1 = bf16[32,32,1024]{2,1,0:T(8,128)(2,1)} custom-call(f32[8,1024,128]{2,1,0:T(8,128)S(1)} %deliver_windows.1.traces_ref), custom_call_target="tpu_custom_call" | custom-call | tf_op jit(solution)/shard_map/place_windows/pallas_call | solution.py:360
Async XLA Ops:
  1.2 1.0 %copy-start = (s32[256,512]{1,0:T(8,128)S(1)}, s32[256,512]{1,0:T(8,128)}, u32[]{:S(2)}) copy-start(s32[256,512]{1,0:T(8,128)} %keep_hbm.1) | copy-start | bytes 1572868
  2.3 0.9 %copy-start.1 = (bf16[256,512]{1,0:T(8,128)(2,1)S(1)}, bf16[256,512]{1,0:T(8,128)(2,1)}, u32[]{:S(2)}) copy-start(bf16[256,512]{1,0:T(8,128)(2,1)} %constant.5.clone.turn_hbm) | copy-start | bytes 786436
  3.2 0.7 %copy-start.2 = (s32[16]{0:T(128)S(1)}, s32[16]{0:T(128)}, u32[]{:S(2)}) copy-start(s32[16]{0:T(128)} %onset_ref.1) | copy-start | bytes 196
  3.9 0.7 %copy-start.3 = (s32[16]{0:T(128)S(1)}, s32[16]{0:T(128)}, u32[]{:S(2)}) copy-start(s32[16]{0:T(128)} %place_ref.1) | copy-start | bytes 196
